TPU v7x, 512 devices: a whole 4x4x16 slice. The times are simulated.
512 devices in a mesh: gx: 8 (over y, core), gy: 4 (over x), gz: 16 (over z).
Axes of the slice: x: 4, y: 4, z: 16, core: 2. Of those that a mesh axis runs over, the one named last changes fastest.
Arguments:
- level_set: float32 [128, 64, 2048], P('gx', 'gy', 'gz'), may hold values from 0 to 1
- velocity: float32 [3, 128, 64, 2048], P(None, 'gx', 'gy', 'gz'), may hold values from -6 to 6
- source: float32 [128, 64, 2048], P('gx', 'gy', 'gz'), may hold values from -6 to 6
- coarse_factor: float32 [512, 512], P(('gx', 'gy', 'gz')), may hold values from -0.2 to 0.2
Outputs:
- level_set_new: float32 [128, 64, 2048], P('gx', 'gy', 'gz')
- pressure: float32 [128, 64, 2048], P('gx', 'gy', 'gz')
All inputs are finite; a program needn't handle non-finite values.
Results may differ from a plain program's by a relative error of at most 0.029.
Values sent between devices are 32-bit elements; how exact they have to be, the bound alone decides.
A program may use at most 64 MiB of HBM per device.

v0:
```python
import jax
import jax.numpy as jnp
import numpy as np
from jax import lax
from jax.sharding import PartitionSpec as P

NP = 8
RSWEEPS = 2
ITERS = 6
GLL_POINTS = (
    -1.0,
    -0.8717401485096066,
    -0.5917001814331423,
    -0.2092992179024789,
    0.2092992179024789,
    0.5917001814331423,
    0.8717401485096066,
    1.0,
)
GLL_WEIGHTS = (
    0.03571428571428571,
    0.21070422714350603,
    0.3411226924835044,
    0.4124587946587038,
    0.4124587946587038,
    0.3411226924835044,
    0.21070422714350603,
    0.03571428571428571,
)
HIGHEST = lax.Precision.HIGHEST
TIME_STEP = 0.02
PSEUDO_STEP = 0.004
INTERFACE_WIDTH = 0.5
GAS_DENSITY = 0.1
SOURCE_SCALE = 20.0


def extended(cells, sides, width):
    for axis, dim in sides:
        count = lax.axis_size(axis)
        ends = count - 1
        head = lax.slice_in_dim(cells, 0, width, axis=dim)
        tail = lax.slice_in_dim(cells, cells.shape[dim] - width, cells.shape[dim], axis=dim)
        cells = jnp.concatenate(
            [
                lax.ppermute(tail, axis, [(i, (i + 1) % count) for i in range(ends)]),
                cells,
                lax.ppermute(head, axis, [((i + 1) % count, i) for i in range(ends)]),
            ],
            axis=dim,
        )
    return cells


def node_tables():
    points = np.array(GLL_POINTS)
    amount = points.shape[0]
    barycentric = np.ones(amount)
    for target in range(amount):
        for partner in range(amount):
            if partner != target:
                barycentric[target] = barycentric[target] / (points[target] - points[partner])
    derivative = np.zeros((amount, amount))
    for target in range(amount):
        for partner in range(amount):
            if partner != target:
                derivative[target, partner] = (
                    barycentric[partner] / barycentric[target] / (points[target] - points[partner])
                )
        derivative[target, target] = -np.sum(derivative[target])
    return derivative


def apply_axis(values, matrix, which_axis):
    if which_axis == 0:
        return jnp.einsum("ap,pqr->aqr", matrix, values, precision=HIGHEST)
    if which_axis == 1:
        return jnp.einsum("aq,pqr->par", matrix, values, precision=HIGHEST)
    return jnp.einsum("pqr,ar->pqa", values, matrix, precision=HIGHEST)


def edge_passes(padded):
    summed = padded
    for which_axis in (1, 2, 3):
        amount = summed.shape[which_axis] - 2
        center = lax.slice_in_dim(summed, 1, amount + 1, axis=which_axis)
        upper_side = lax.slice_in_dim(summed, 2, amount + 2, axis=which_axis)
        lower_side = lax.slice_in_dim(summed, 0, amount, axis=which_axis)
        shape_list = [1, 1, 1, 1]
        shape_list[which_axis] = amount
        position = (jnp.arange(amount) % NP).reshape(shape_list)
        summed = (
            center
            + jnp.where(position == NP - 1, upper_side, 0.0)
            + jnp.where(position == 0, lower_side, 0.0)
        )
    return summed


def assemble(stacked):
    padded = extended(stacked, (("gx", 1), ("gy", 2), ("gz", 3)), 1)
    return edge_passes(padded)


def body(level_set, velocity, source, coarse_factor):
    shape_tuple = level_set.shape
    derivative = node_tables()
    deriv_tables = [
        jnp.asarray(np.kron(np.eye(extent // NP), derivative), jnp.float32)
        for extent in shape_tuple
    ]
    trans_tables = [
        jnp.asarray(np.kron(np.eye(extent // NP), derivative.T), jnp.float32)
        for extent in shape_tuple
    ]
    square_tables = [
        jnp.asarray(np.kron(np.eye(extent // NP), (derivative * derivative).T), jnp.float32)
        for extent in shape_tuple
    ]
    weights = jnp.asarray(np.array(GLL_WEIGHTS), jnp.float32)
    along_x = jnp.tile(weights, shape_tuple[0] // NP)
    along_y = jnp.tile(weights, shape_tuple[1] // NP)
    along_z = jnp.tile(weights, shape_tuple[2] // NP)
    bmass = along_x[:, None, None] * along_y[None, :, None] * along_z[None, None, :]
    gradient = [
        apply_axis(level_set, deriv_tables[which_axis], which_axis) for which_axis in range(3)
    ]
    advect = velocity[0] * gradient[0] + velocity[1] * gradient[1] + velocity[2] * gradient[2]
    divergence = (
        apply_axis(bmass * velocity[0], trans_tables[0], 0)
        + apply_axis(bmass * velocity[1], trans_tables[1], 1)
        + apply_axis(bmass * velocity[2], trans_tables[2], 2)
        + bmass * source
    )
    assembled = assemble(jnp.stack([bmass * advect, bmass, divergence]))
    mass_sum = assembled[1]
    weight = bmass / mass_sum
    level_now = level_set - TIME_STEP * assembled[0] / mass_sum
    rhs_field = SOURCE_SCALE * assembled[2]
    for sweep in range(RSWEEPS):
        gradient = [
            apply_axis(level_now, deriv_tables[which_axis], which_axis) for which_axis in range(3)
        ]
        inv_norm = 1.0 / jnp.sqrt(
            1.0 + gradient[0] * gradient[0] + gradient[1] * gradient[1] + gradient[2] * gradient[2]
        )
        compress = level_now * (1.0 - level_now) * inv_norm
        weak_form = apply_axis(
            bmass * (compress * gradient[0] - INTERFACE_WIDTH * gradient[0]), trans_tables[0], 0
        )
        weak_form = weak_form + apply_axis(
            bmass * (compress * gradient[1] - INTERFACE_WIDTH * gradient[1]), trans_tables[1], 1
        )
        weak_form = weak_form + apply_axis(
            bmass * (compress * gradient[2] - INTERFACE_WIDTH * gradient[2]), trans_tables[2], 2
        )
        level_now = level_now + PSEUDO_STEP * assemble(weak_form[None])[0] / mass_sum
    inverse_density = 1.0 / (GAS_DENSITY + (1.0 - GAS_DENSITY) * jnp.clip(level_now, 0.0, 1.0))
    scaled = bmass * inverse_density
    diag_local = (
        apply_axis(scaled, square_tables[0], 0)
        + apply_axis(scaled, square_tables[1], 1)
        + apply_axis(scaled, square_tables[2], 2)
        + bmass
    )
    diagonal = assemble(diag_local[None])[0]
    own_row = coarse_factor[0]

    def precondition(residual):
        jacobi = residual / diagonal
        restricted = jnp.sum(weight * residual)
        coarse_mid = lax.psum(restricted * own_row, ("gx", "gy", "gz"))
        coarse_value = jnp.dot(own_row, coarse_mid, precision=HIGHEST)
        result = jacobi + assemble((weight * coarse_value)[None])[0]
        return (result, lax.psum(jnp.sum(weight * residual * result), ("gx", "gy", "gz")))

    pressure = jnp.zeros_like(rhs_field)
    residual = rhs_field
    direction, inner_now = precondition(residual)
    for step in range(ITERS):
        local_part = bmass * direction
        for element_which_axis in range(3):
            local_part = local_part + apply_axis(
                scaled
                * apply_axis(direction, deriv_tables[element_which_axis], element_which_axis),
                trans_tables[element_which_axis],
                element_which_axis,
            )
        image = assemble(local_part[None])[0]
        curvature = lax.psum(jnp.sum(weight * direction * image), ("gx", "gy", "gz"))
        step_size = inner_now / curvature
        pressure = pressure + step_size * direction
        residual = residual - step_size * image
        if step + 1 < ITERS:
            preconditioned, inner_next = precondition(residual)
            direction = preconditioned + inner_next / inner_now * direction
            inner_now = inner_next
    return (level_now, pressure)


def solution(mesh):
    in_specs = (
        P("gx", "gy", "gz"),
        P(None, "gx", "gy", "gz"),
        P("gx", "gy", "gz"),
        P(("gx", "gy", "gz"), None),
    )
    out_specs = (P("gx", "gy", "gz"), P("gx", "gy", "gz"))
    return jax.shard_map(body, mesh=mesh, in_specs=in_specs, out_specs=out_specs, check_vma=False)
```

profile of v0, /device:TPU:1, one launch (start us, length us, event | category | flops | bytes accessed | tf_op | source)
XLA Modules:
  0.0 2206.5 jit_solution(12459862347474892173)
XLA Ops:
  6.2 4.6 collective-permute-start
  10.8 5.5 collective-permute-start.1
  63.5 5.4 collective-permute-done.11
  87.6 4.9 collective-permute-start.16
  103.5 104.3 %psum.126 = f32[512]{0:T(512)S(1)} all-reduce(f32[512]{0:T(512)S(1)} %broadcast_multiply_fusion.13), channel_id=1, replica_groups=mesh['gx'=8,'gy'=4,'gz'=16] {'gx','gy','gz'}, use_global_device_ids=true, to_apply=%region_1.2 | all-reduce | flops 512 | bytes 4096 | tf_op jit(solution)/shard_map/psum | solution.py:172
  240.6 4.4 collective-permute-done.23
  256.2 4.3 collective-permute-start.32
  273.4 4.8 collective-permute-done.35
  279.6 104.5 %all-reduce = (f32[]{:T(128)}, f32[]{:T(128)}) all-reduce(f32[]{:T(128)} %get-tuple-element.9, f32[]{:T(128)} %get-tuple-element.8), channel_id=1, replica_groups=mesh['gx'=8,'gy'=4,'gz'=16] {'gx','gy','gz'}, use_global_device_ids=true, to_apply=%region_3.4 | all-reduce | flops 2 | bytes 16 | tf_op jit(solution)/shard_map/psum | solution.py:175
  386.8 98.4 %psum.129 = f32[512]{0:T(512)S(1)} all-reduce(f32[512]{0:T(512)S(1)} %broadcast_multiply_fusion.12), channel_id=1, replica_groups=mesh['gx'=8,'gy'=4,'gz'=16] {'gx','gy','gz'}, use_global_device_ids=true, to_apply=%region_7.8 | all-reduce | flops 512 | bytes 4096 | tf_op jit(solution)/shard_map/psum | solution.py:172
  514.5 101.3 %psum.130 = f32[]{:T(128)} all-reduce(f32[]{:T(128)} %get-tuple-element.36), channel_id=1, replica_groups=mesh['gx'=8,'gy'=4,'gz'=16] {'gx','gy','gz'}, use_global_device_ids=true, to_apply=%region_9.10 | all-reduce | flops 1 | bytes 8 | tf_op jit(solution)/shard_map/psum | solution.py:175
  645.7 102.2 %psum.131 = f32[]{:T(128)} all-reduce(f32[]{:T(128)} %get-tuple-element.34), channel_id=1, replica_groups=mesh['gx'=8,'gy'=4,'gz'=16] {'gx','gy','gz'}, use_global_device_ids=true, to_apply=%region_11.12 | all-reduce | flops 1 | bytes 8 | tf_op jit(solution)/shard_map/psum | solution.py:190
  750.5 99.1 %psum.132 = f32[512]{0:T(512)S(1)} all-reduce(f32[512]{0:T(512)S(1)} %broadcast_multiply_fusion.11), channel_id=1, replica_groups=mesh['gx'=8,'gy'=4,'gz'=16] {'gx','gy','gz'}, use_global_device_ids=true, to_apply=%region_13.14 | all-reduce | flops 512 | bytes 4096 | tf_op jit(solution)/shard_map/psum | solution.py:172
  879.3 100.7 %psum.133 = f32[]{:T(128)} all-reduce(f32[]{:T(128)} %get-tuple-element.30), channel_id=1, replica_groups=mesh['gx'=8,'gy'=4,'gz'=16] {'gx','gy','gz'}, use_global_device_ids=true, to_apply=%region_15.16 | all-reduce | flops 1 | bytes 8 | tf_op jit(solution)/shard_map/psum | solution.py:175
  1009.8 102.3 %psum.134 = f32[]{:T(128)} all-reduce(f32[]{:T(128)} %get-tuple-element.28), channel_id=1, replica_groups=mesh['gx'=8,'gy'=4,'gz'=16] {'gx','gy','gz'}, use_global_device_ids=true, to_apply=%region_17.18 | all-reduce | flops 1 | bytes 8 | tf_op jit(solution)/shard_map/psum | solution.py:190
  1114.7 98.7 %psum.135 = f32[512]{0:T(512)S(1)} all-reduce(f32[512]{0:T(512)S(1)} %broadcast_multiply_fusion.10), channel_id=1, replica_groups=mesh['gx'=8,'gy'=4,'gz'=16] {'gx','gy','gz'}, use_global_device_ids=true, to_apply=%region_19.20 | all-reduce | flops 512 | bytes 4096 | tf_op jit(solution)/shard_map/psum | solution.py:172
  1243.1 100.7 %psum.136 = f32[]{:T(128)} all-reduce(f32[]{:T(128)} %get-tuple-element.24), channel_id=1, replica_groups=mesh['gx'=8,'gy'=4,'gz'=16] {'gx','gy','gz'}, use_global_device_ids=true, to_apply=%region_21.22 | all-reduce | flops 1 | bytes 8 | tf_op jit(solution)/shard_map/psum | solution.py:175
  1373.6 102.5 %psum.137 = f32[]{:T(128)} all-reduce(f32[]{:T(128)} %get-tuple-element.22), channel_id=1, replica_groups=mesh['gx'=8,'gy'=4,'gz'=16] {'gx','gy','gz'}, use_global_device_ids=true, to_apply=%region_23.24 | all-reduce | flops 1 | bytes 8 | tf_op jit(solution)/shard_map/psum | solution.py:190
  1478.7 98.7 %psum.138 = f32[512]{0:T(512)S(1)} all-reduce(f32[512]{0:T(512)S(1)} %broadcast_multiply_fusion.9), channel_id=1, replica_groups=mesh['gx'=8,'gy'=4,'gz'=16] {'gx','gy','gz'}, use_global_device_ids=true, to_apply=%region_25.26 | all-reduce | flops 512 | bytes 4096 | tf_op jit(solution)/shard_map/psum | solution.py:172
  1607.0 100.7 %psum.139 = f32[]{:T(128)} all-reduce(f32[]{:T(128)} %get-tuple-element.18), channel_id=1, replica_groups=mesh['gx'=8,'gy'=4,'gz'=16] {'gx','gy','gz'}, use_global_device_ids=true, to_apply=%region_27.28 | all-reduce | flops 1 | bytes 8 | tf_op jit(solution)/shard_map/psum | solution.py:175
  1737.5 102.3 %psum.140 = f32[]{:T(128)} all-reduce(f32[]{:T(128)} %get-tuple-element.16), channel_id=1, replica_groups=mesh['gx'=8,'gy'=4,'gz'=16] {'gx','gy','gz'}, use_global_device_ids=true, to_apply=%region_29.30 | all-reduce | flops 1 | bytes 8 | tf_op jit(solution)/shard_map/psum | solution.py:190
  1842.5 98.7 %psum.141 = f32[512]{0:T(512)S(1)} all-reduce(f32[512]{0:T(512)S(1)} %broadcast_multiply_fusion.8), channel_id=1, replica_groups=mesh['gx'=8,'gy'=4,'gz'=16] {'gx','gy','gz'}, use_global_device_ids=true, to_apply=%region_31.32 | all-reduce | flops 512 | bytes 4096 | tf_op jit(solution)/shard_map/psum | solution.py:172
  1970.8 100.7 %psum.142 = f32[]{:T(128)} all-reduce(f32[]{:T(128)} %get-tuple-element.12), channel_id=1, replica_groups=mesh['gx'=8,'gy'=4,'gz'=16] {'gx','gy','gz'}, use_global_device_ids=true, to_apply=%region_33.34 | all-reduce | flops 1 | bytes 8 | tf_op jit(solution)/shard_map/psum | solution.py:175
  2102.2 102.1 %psum.143 = f32[]{:T(128)} all-reduce(f32[]{:T(128)} %fusion.92), channel_id=1, replica_groups=mesh['gx'=8,'gy'=4,'gz'=16] {'gx','gy','gz'}, use_global_device_ids=true, to_apply=%region_35.36 | all-reduce | flops 1 | bytes 8 | tf_op jit(solution)/shard_map/psum | solution.py:190
  (437 shorter events, 436.9 us)
Async XLA Ops:
  6.2 10.1 collective-permute-start
  54.7 8.8 collective-permute-start.10
  58.3 10.6 collective-permute-start.11
  87.6 10.1 collective-permute-start.16
  92.5 9.1 collective-permute-start.17
  209.1 10.4 collective-permute-start.24
  214.4 8.8 collective-permute-start.18
  219.6 9.2 collective-permute-start.26
  231.8 8.8 collective-permute-start.22
  235.7 9.3 collective-permute-start.23
  268.2 10.0 collective-permute-start.35
  500.5 8.7 collective-permute-start.40
  504.2 8.9 collective-permute-start.41
  635.3 9.1 collective-permute-start.47
  865.3 8.7 collective-permute-start.52
  869.0 8.9 collective-permute-start.53
  999.4 9.1 collective-permute-start.59
  1229.1 8.7 collective-permute-start.64
  1232.8 8.9 collective-permute-start.65
  1363.2 9.1 collective-permute-start.71
  1596.8 8.9 collective-permute-start.77
  1727.1 9.1 collective-permute-start.83
  1960.6 8.9 collective-permute-start.89
  2091.0 9.1 collective-permute-start.95
  (81 other events, 617.3 us)
where the time goes:
time: 2220 us; the launch traced here: 2210 us
  blocking collectives  1720 us (77%)
  starting transfers between devices  211 us (10%)
  waiting for transfers between devices  199 us (9%)
  other arithmetic  36.4 us (2%)
    psum x6, blocking collectives, precondition(): lax.psum(jnp.sum(weight * residual * result), ('gx', 'gy', 'gz'))  609 us
    psum x6, blocking collectives, precondition(): coarse_mid = lax.psum(restricted * own_row, ('gx', 'gy', 'gz'))  598 us
    psum x5, blocking collectives, body(): lax.psum(jnp.sum(weight * direction * image), ('gx', 'gy', 'gz'))  511 us
    ppermute x48, waiting for transfers between devices, extended(): lax.ppermute(head, axis, [((i + 1) % count, i) for i in range(ends)])  147 us
    ppermute x48, starting transfers between devices, extended(): lax.ppermute(tail, axis, [(i, (i + 1) % count) for i in range(ends)])  133 us
    ppermute x48, starting transfers between devices, extended(): lax.ppermute(head, axis, [((i + 1) % count, i) for i in range(ends)])  77.4 us
    ppermute x48, waiting for transfers between devices, extended(): lax.ppermute(tail, axis, [(i, (i + 1) % count) for i in range(ends)])  51.5 us
  transfers between devices with their start and end apart: 96, of which 59 were waited for; matrix products, arithmetic and copies ran while one was open for 0% of the time, Pallas kernels for 0%

commit v1 on v0

--- a/solution.py
+++ b/solution.py
@@ -169,7 +169,9 @@
     def precondition(residual):
         jacobi = residual / diagonal
         restricted = jnp.sum(weight * residual)
-        coarse_mid = lax.psum(restricted * own_row, ("gx", "gy", "gz"))
+        coarse_mid = restricted * own_row
+        for mesh_axis in (("gy", "gz"), "gx"):
+            coarse_mid = lax.psum(coarse_mid, mesh_axis)
         coarse_value = jnp.dot(own_row, coarse_mid, precision=HIGHEST)
         result = jacobi + assemble((weight * coarse_value)[None])[0]
         return (result, lax.psum(jnp.sum(weight * residual * result), ("gx", "gy", "gz")))

time: 2220 us -> 2500 us (1.13)
  blocking collectives: 1720 us -> 2010 us
    psum x6 -> x12, blocking collectives: 598 us -> 918 us  [precondition(): coarse_mid = lax.psum(coarse_mid, mesh_axis)]
where the time goes in v1:
time: 2500 us; the launch traced here: 2480 us
  blocking collectives  2010 us (80%)
  starting transfers between devices  200 us (8%)
  waiting for transfers between devices  195 us (8%)
  other arithmetic  36.4 us (1%)
    psum x12, blocking collectives, precondition(): coarse_mid = lax.psum(coarse_mid, mesh_axis)  918 us
    psum x6, blocking collectives, precondition(): lax.psum(jnp.sum(weight * residual * result), ('gx', 'gy', 'gz'))  593 us
    psum x5, blocking collectives, body(): lax.psum(jnp.sum(weight * direction * image), ('gx', 'gy', 'gz'))  499 us
    ppermute x48, waiting for transfers between devices, extended(): lax.ppermute(head, axis, [((i + 1) % count, i) for i in range(ends)])  143 us
    ppermute x48, starting transfers between devices, extended(): lax.ppermute(tail, axis, [(i, (i + 1) % count) for i in range(ends)])  120 us
    ppermute x48, starting transfers between devices, extended(): lax.ppermute(head, axis, [((i + 1) % count, i) for i in range(ends)])  80.2 us
    ppermute x48, waiting for transfers between devices, extended(): lax.ppermute(tail, axis, [(i, (i + 1) % count) for i in range(ends)])  51.8 us
  transfers between devices with their start and end apart: 96, of which 59 were waited for; matrix products, arithmetic and copies ran while one was open for 0% of the time, Pallas kernels for 0%

profile of v1, /device:TPU:1, one launch (start us, length us, event | category | flops | bytes accessed | tf_op | source)
XLA Modules:
  0.0 2483.8 jit_solution(1696016323225068927)
XLA Ops:
  10.8 5.5 collective-permute-start.1
  103.5 112.0 %psum.168 = f32[512]{0:T(512)S(1)} all-reduce(f32[512]{0:T(512)S(1)} %broadcast_multiply_fusion.13), channel_id=1, replica_groups=mesh['gx'=8,'gy'=4,'gz'=16] {'gy','gz'}, use_global_device_ids=true, to_apply=%region_1.2 | all-reduce | flops 512 | bytes 4096 | tf_op jit(solution)/shard_map/psum | solution.py:174
  215.5 40.3 %psum.169 = f32[512]{0:T(512)S(1)} all-reduce(f32[512]{0:T(512)S(1)} %psum.168), channel_id=1, replica_groups=mesh['gx'=8,'gy'=4,'gz'=16] {'gx'}, use_global_device_ids=true, to_apply=%region_2.3 | all-reduce | flops 512 | bytes 4096 | tf_op jit(solution)/shard_map/psum | solution.py:174
  324.4 99.5 %all-reduce = (f32[]{:T(128)}, f32[]{:T(128)}) all-reduce(f32[]{:T(128)} %get-tuple-element.9, f32[]{:T(128)} %get-tuple-element.8), channel_id=1, replica_groups=mesh['gx'=8,'gy'=4,'gz'=16] {'gx','gy','gz'}, use_global_device_ids=true, to_apply=%region_4.5 | all-reduce | flops 2 | bytes 16 | tf_op jit(solution)/shard_map/psum | solution.py:177
  426.6 112.2 %psum.172 = f32[512]{0:T(512)S(1)} all-reduce(f32[512]{0:T(512)S(1)} %broadcast_multiply_fusion.12), channel_id=1, replica_groups=mesh['gx'=8,'gy'=4,'gz'=16] {'gy','gz'}, use_global_device_ids=true, to_apply=%region_8.9 | all-reduce | flops 512 | bytes 4096 | tf_op jit(solution)/shard_map/psum | solution.py:174
  538.7 40.3 %psum.173 = f32[512]{0:T(512)S(1)} all-reduce(f32[512]{0:T(512)S(1)} %psum.172), channel_id=1, replica_groups=mesh['gx'=8,'gy'=4,'gz'=16] {'gx'}, use_global_device_ids=true, to_apply=%region_9.10 | all-reduce | flops 512 | bytes 4096 | tf_op jit(solution)/shard_map/psum | solution.py:174
  605.1 98.6 %psum.174 = f32[]{:T(128)} all-reduce(f32[]{:T(128)} %get-tuple-element.36), channel_id=1, replica_groups=mesh['gx'=8,'gy'=4,'gz'=16] {'gx','gy','gz'}, use_global_device_ids=true, to_apply=%region_11.12 | all-reduce | flops 1 | bytes 8 | tf_op jit(solution)/shard_map/psum | solution.py:177
  734.8 99.7 %psum.175 = f32[]{:T(128)} all-reduce(f32[]{:T(128)} %get-tuple-element.34), channel_id=1, replica_groups=mesh['gx'=8,'gy'=4,'gz'=16] {'gx','gy','gz'}, use_global_device_ids=true, to_apply=%region_13.14 | all-reduce | flops 1 | bytes 8 | tf_op jit(solution)/shard_map/psum | solution.py:192
  837.2 113.0 %psum.176 = f32[512]{0:T(512)S(1)} all-reduce(f32[512]{0:T(512)S(1)} %broadcast_multiply_fusion.11), channel_id=1, replica_groups=mesh['gx'=8,'gy'=4,'gz'=16] {'gy','gz'}, use_global_device_ids=true, to_apply=%region_15.16 | all-reduce | flops 512 | bytes 4096 | tf_op jit(solution)/shard_map/psum | solution.py:174
  950.2 40.3 %psum.177 = f32[512]{0:T(512)S(1)} all-reduce(f32[512]{0:T(512)S(1)} %psum.176), channel_id=1, replica_groups=mesh['gx'=8,'gy'=4,'gz'=16] {'gx'}, use_global_device_ids=true, to_apply=%region_16.17 | all-reduce | flops 512 | bytes 4096 | tf_op jit(solution)/shard_map/psum | solution.py:174
  1016.4 98.9 %psum.178 = f32[]{:T(128)} all-reduce(f32[]{:T(128)} %get-tuple-element.30), channel_id=1, replica_groups=mesh['gx'=8,'gy'=4,'gz'=16] {'gx','gy','gz'}, use_global_device_ids=true, to_apply=%region_18.19 | all-reduce | flops 1 | bytes 8 | tf_op jit(solution)/shard_map/psum | solution.py:177
  1146.4 99.7 %psum.179 = f32[]{:T(128)} all-reduce(f32[]{:T(128)} %get-tuple-element.28), channel_id=1, replica_groups=mesh['gx'=8,'gy'=4,'gz'=16] {'gx','gy','gz'}, use_global_device_ids=true, to_apply=%region_20.21 | all-reduce | flops 1 | bytes 8 | tf_op jit(solution)/shard_map/psum | solution.py:192
  1248.8 113.0 %psum.180 = f32[512]{0:T(512)S(1)} all-reduce(f32[512]{0:T(512)S(1)} %broadcast_multiply_fusion.10), channel_id=1, replica_groups=mesh['gx'=8,'gy'=4,'gz'=16] {'gy','gz'}, use_global_device_ids=true, to_apply=%region_22.23 | all-reduce | flops 512 | bytes 4096 | tf_op jit(solution)/shard_map/psum | solution.py:174
  1361.8 40.3 %psum.181 = f32[512]{0:T(512)S(1)} all-reduce(f32[512]{0:T(512)S(1)} %psum.180), channel_id=1, replica_groups=mesh['gx'=8,'gy'=4,'gz'=16] {'gx'}, use_global_device_ids=true, to_apply=%region_23.24 | all-reduce | flops 512 | bytes 4096 | tf_op jit(solution)/shard_map/psum | solution.py:174
  1428.1 98.7 %psum.182 = f32[]{:T(128)} all-reduce(f32[]{:T(128)} %get-tuple-element.24), channel_id=1, replica_groups=mesh['gx'=8,'gy'=4,'gz'=16] {'gx','gy','gz'}, use_global_device_ids=true, to_apply=%region_25.26 | all-reduce | flops 1 | bytes 8 | tf_op jit(solution)/shard_map/psum | solution.py:177
  1557.9 99.7 %psum.183 = f32[]{:T(128)} all-reduce(f32[]{:T(128)} %get-tuple-element.22), channel_id=1, replica_groups=mesh['gx'=8,'gy'=4,'gz'=16] {'gx','gy','gz'}, use_global_device_ids=true, to_apply=%region_27.28 | all-reduce | flops 1 | bytes 8 | tf_op jit(solution)/shard_map/psum | solution.py:192
  1660.3 113.0 %psum.184 = f32[512]{0:T(512)S(1)} all-reduce(f32[512]{0:T(512)S(1)} %broadcast_multiply_fusion.9), channel_id=1, replica_groups=mesh['gx'=8,'gy'=4,'gz'=16] {'gy','gz'}, use_global_device_ids=true, to_apply=%region_29.30 | all-reduce | flops 512 | bytes 4096 | tf_op jit(solution)/shard_map/psum | solution.py:174
  1773.3 40.3 %psum.185 = f32[512]{0:T(512)S(1)} all-reduce(f32[512]{0:T(512)S(1)} %psum.184), channel_id=1, replica_groups=mesh['gx'=8,'gy'=4,'gz'=16] {'gx'}, use_global_device_ids=true, to_apply=%region_30.31 | all-reduce | flops 512 | bytes 4096 | tf_op jit(solution)/shard_map/psum | solution.py:174
  1839.5 98.9 %psum.186 = f32[]{:T(128)} all-reduce(f32[]{:T(128)} %get-tuple-element.18), channel_id=1, replica_groups=mesh['gx'=8,'gy'=4,'gz'=16] {'gx','gy','gz'}, use_global_device_ids=true, to_apply=%region_32.33 | all-reduce | flops 1 | bytes 8 | tf_op jit(solution)/shard_map/psum | solution.py:177
  1969.6 99.7 %psum.187 = f32[]{:T(128)} all-reduce(f32[]{:T(128)} %get-tuple-element.16), channel_id=1, replica_groups=mesh['gx'=8,'gy'=4,'gz'=16] {'gx','gy','gz'}, use_global_device_ids=true, to_apply=%region_34.35 | all-reduce | flops 1 | bytes 8 | tf_op jit(solution)/shard_map/psum | solution.py:192
  2072.0 113.0 %psum.188 = f32[512]{0:T(512)S(1)} all-reduce(f32[512]{0:T(512)S(1)} %broadcast_multiply_fusion.8), channel_id=1, replica_groups=mesh['gx'=8,'gy'=4,'gz'=16] {'gy','gz'}, use_global_device_ids=true, to_apply=%region_36.37 | all-reduce | flops 512 | bytes 4096 | tf_op jit(solution)/shard_map/psum | solution.py:174
  2185.0 40.3 %psum.189 = f32[512]{0:T(512)S(1)} all-reduce(f32[512]{0:T(512)S(1)} %psum.188), channel_id=1, replica_groups=mesh['gx'=8,'gy'=4,'gz'=16] {'gx'}, use_global_device_ids=true, to_apply=%region_37.38 | all-reduce | flops 512 | bytes 4096 | tf_op jit(solution)/shard_map/psum | solution.py:174
  2251.2 98.7 %psum.190 = f32[]{:T(128)} all-reduce(f32[]{:T(128)} %get-tuple-element.12), channel_id=1, replica_groups=mesh['gx'=8,'gy'=4,'gz'=16] {'gx','gy','gz'}, use_global_device_ids=true, to_apply=%region_39.40 | all-reduce | flops 1 | bytes 8 | tf_op jit(solution)/shard_map/psum | solution.py:177
  2381.8 99.7 %psum.191 = f32[]{:T(128)} all-reduce(f32[]{:T(128)} %fusion.92), channel_id=1, replica_groups=mesh['gx'=8,'gy'=4,'gz'=16] {'gx','gy','gz'}, use_global_device_ids=true, to_apply=%region_41.42 | all-reduce | flops 1 | bytes 8 | tf_op jit(solution)/shard_map/psum | solution.py:192
  (443 shorter events, 450.5 us)
Async XLA Ops:
  6.2 10.1 collective-permute-start
  58.3 10.6 collective-permute-start.11
  87.6 10.1 collective-permute-start.16
  92.5 9.1 collective-permute-start.17
  257.2 10.3 collective-permute-start.24
  275.7 9.0 collective-permute-start.28
  277.4 9.2 collective-permute-start.29
  278.9 9.0 collective-permute-start.22
  282.9 8.9 collective-permute-start.23
  314.0 9.1 collective-permute-start.35
  594.8 8.9 collective-permute-start.41
  720.7 8.9 collective-permute-start.46
  724.4 9.1 collective-permute-start.47
  1006.0 9.1 collective-permute-start.53
  1132.3 8.9 collective-permute-start.58
  1136.0 9.1 collective-permute-start.59
  1417.6 9.1 collective-permute-start.65
  1543.8 8.9 collective-permute-start.70
  1547.5 9.1 collective-permute-start.71
  1829.1 9.1 collective-permute-start.77
  1955.5 8.9 collective-permute-start.82
  1959.2 9.1 collective-permute-start.83
  2240.7 9.1 collective-permute-start.89
  2370.6 9.1 collective-permute-start.95
  (81 other events, 700.7 us)
